TPU v7x, 32 devices: a whole 2x2x4 slice. The times are simulated.
32 devices in a mesh: section: 2 (over x), dp: 16 (over z, y, core).
Axes of the slice: x: 2, y: 2, z: 4, core: 2. Of those that a mesh axis runs over, the one named last changes fastest.
Arguments:
- section_inputs: bfloat16 [2, 2048, 8192], P('section', 'dp'), may hold values from -6 to 6
- teacher_states: bfloat16 [2048, 8192], P('dp'), may hold values from -6 to 6
- confidence: int32 [2048], P('dp'), may hold values from 1 to 256
- gains: float32 [2, 8192], P('section'), may hold values from 0.1 to 1.9
- w_down: bfloat16 [2, 8192, 256], P('section', 'dp'), may hold values from -0.0625 to 0.0625
- w_up: bfloat16 [2, 8192, 256], P('section', 'dp'), may hold values from -0.375 to 0.375
Outputs:
- input_grads: bfloat16 [2, 2048, 8192], P('section', 'dp')
- grad_down: float32 [2, 8192, 256], P('section', 'dp')
- grad_up: float32 [2, 8192, 256], P('section', 'dp')
- grad_gain: float32 [2, 8192], P('section', 'dp')
All inputs are finite; a program needn't handle non-finite values.
Results may differ from a plain program's by a relative error of at most 0.013.
Values may be sent and summed in bfloat16 or wider, within the bound.
No kernel may reach another device: no remote copies, remote signals or barrier semaphores. Data moves between devices by JAX's collectives and lax.ppermute only.
A program may use at most 64 MiB of HBM per device.

v0:
```python
import jax
import jax.numpy as jnp
from jax import lax
from jax.sharding import PartitionSpec as P

MICRO = 4
ROWS = 32
TOK_DEV = 128
EPSILON = 1e-05


def shifted(block, axis, distance):
    devices = range(lax.axis_size(axis))
    route = [(i - distance, i) for i in devices if i - distance in devices]
    return lax.ppermute(block, axis, route)


def write_rows(buffer, fresh, first_row, active_step):
    previous = lax.dynamic_slice_in_dim(buffer, first_row, fresh.shape[0], 0)
    return lax.dynamic_update_slice_in_dim(
        buffer, jnp.where(active_step, fresh, previous), first_row, 0
    )


def local(section_inputs, teacher_states, confidence, gains, w_down, w_up):
    sections = lax.axis_size("section")
    section_index = lax.axis_index("section")
    layer_inputs = section_inputs[0]
    gain = gains[0]
    down_matrix, up_matrix = (
        lax.all_gather(w_down[0], "dp", axis=0, tiled=True),
        lax.all_gather(w_up[0], "dp", axis=0, tiled=True),
    )
    is_last = section_index == sections - 1
    rank_width = down_matrix.shape[1]
    width = down_matrix.shape[0]

    def run_step(step_index, carry):
        incoming, scaled_all, cot_all, pre_all, hidden_all, grads_all, gain_term = carry
        micro_index = step_index - (sections - 1 - section_index)
        active_step = (micro_index >= 0) & (micro_index < MICRO)
        first_row = jnp.clip(micro_index, 0, MICRO - 1) * ROWS
        rows_in = lax.dynamic_slice_in_dim(layer_inputs, first_row, ROWS, 0)
        teacher_rows = lax.dynamic_slice_in_dim(teacher_states, first_row, ROWS, 0)
        weight_rows = (
            lax.dynamic_slice_in_dim(confidence, first_row, ROWS, 0).astype(jnp.float32) / 256.0
        )
        values = rows_in.astype(jnp.float32)
        inverse = lax.rsqrt(jnp.mean(values * values, axis=-1, keepdims=True) + EPSILON)
        normed = values * inverse
        scaled = (normed * gain).astype(jnp.bfloat16)
        preact = jnp.dot(scaled, down_matrix, preferred_element_type=jnp.float32)
        hidden = jax.nn.silu(preact).astype(jnp.bfloat16)
        branch = jnp.einsum("tr,dr->td", hidden, up_matrix, preferred_element_type=jnp.float32)
        top_grad = (
            weight_rows[:, None] * (values + branch - teacher_rows.astype(jnp.float32))
        ).astype(jnp.bfloat16)
        cotangent = jnp.where(is_last, top_grad, incoming)
        hidden_grad = jnp.dot(cotangent, up_matrix, preferred_element_type=jnp.float32)
        sigmoid_val = jax.nn.sigmoid(preact)
        pre_grad = (hidden_grad * sigmoid_val * (1.0 + preact * (1.0 - sigmoid_val))).astype(
            jnp.bfloat16
        )
        normed_grad = jnp.einsum(
            "tr,dr->td", pre_grad, down_matrix, preferred_element_type=jnp.float32
        )
        scaled_grad = normed_grad * gain
        input_grad = cotangent.astype(jnp.float32) + inverse * (
            scaled_grad - normed * jnp.mean(scaled_grad * normed, axis=-1, keepdims=True)
        )
        input_grad = input_grad.astype(jnp.bfloat16)
        gain_term = gain_term + jnp.where(active_step, jnp.sum(normed_grad * normed, axis=0), 0.0)
        scaled_all = write_rows(scaled_all, scaled, first_row, active_step)
        cot_all = write_rows(cot_all, cotangent, first_row, active_step)
        pre_all = write_rows(pre_all, pre_grad, first_row, active_step)
        hidden_all = write_rows(hidden_all, hidden, first_row, active_step)
        grads_all = write_rows(grads_all, input_grad, first_row, active_step)
        outgoing = shifted(input_grad, "section", -1)
        return (outgoing, scaled_all, cot_all, pre_all, hidden_all, grads_all, gain_term)

    token_count = layer_inputs.shape[0]
    start_carry = (
        jnp.zeros((ROWS, width), jnp.bfloat16),
        jnp.zeros((token_count, width), jnp.bfloat16),
        jnp.zeros((token_count, width), jnp.bfloat16),
        jnp.zeros((token_count, rank_width), jnp.bfloat16),
        jnp.zeros((token_count, rank_width), jnp.bfloat16),
        jnp.zeros((token_count, width), jnp.bfloat16),
        jnp.zeros((width,), jnp.float32),
    )
    final_carry = lax.fori_loop(0, MICRO + sections - 1, run_step, start_carry)
    _, scaled_all, cot_all, pre_all, hidden_all, grads_all, gain_term = final_carry
    down_part = jnp.einsum("td,tr->dr", scaled_all, pre_all, preferred_element_type=jnp.float32)
    up_part = jnp.einsum("td,tr->dr", cot_all, hidden_all, preferred_element_type=jnp.float32)
    stacked = lax.psum_scatter(
        jnp.concatenate([down_part, up_part], axis=1).astype(jnp.bfloat16),
        "dp",
        scatter_dimension=0,
        tiled=True,
    ).astype(jnp.float32)
    gain_sum = lax.psum_scatter(gain_term, "dp", scatter_dimension=0, tiled=True)
    stacked = stacked / TOK_DEV
    grad_down = stacked[:, :rank_width]
    grad_up = stacked[:, rank_width:]
    return (grads_all[None], grad_down[None], grad_up[None], (gain_sum / TOK_DEV)[None])


def solution(mesh):
    in_specs = (
        P("section", "dp", None),
        P("dp", None),
        P("dp"),
        P("section", None),
        P("section", "dp", None),
        P("section", "dp", None),
    )
    out_specs = (
        P("section", "dp", None),
        P("section", "dp", None),
        P("section", "dp", None),
        P("section", "dp"),
    )
    return jax.shard_map(local, mesh=mesh, in_specs=in_specs, out_specs=out_specs, check_vma=False)
```

profile of v0, /device:TPU:0, one launch (start us, length us, event | category | flops | bytes accessed | tf_op | source)
XLA Modules:
  0.0 383.3 jit_solution(15505079731274536532)
XLA Ops:
  8.7 54.7 %all-gather.5.cloned.1.call-done = bf16[1,8192,256]{2,1,0:T(8,128)(2,1)} async-done(((bf16[1,512,256]{2,1,0:T(8,128)(2,1)}), bf16[1,8192,256]{2,1,0:T(8,128)(2,1)}) %all-gather.5.cloned.1.call-update) | async-done | bytes 4194320 | tf_op jit(solution)/shard_map/all_gather | solution.py:31
  63.5 51.2 %all-gather.7.cloned.1.call-done = bf16[1,8192,256]{2,1,0:T(8,128)(2,1)} async-done(((bf16[1,512,256]{2,1,0:T(8,128)(2,1)}), bf16[1,8192,256]{2,1,0:T(8,128)(2,1)}) %all-gather.7.cloned.1.call-update) | async-done | bytes 4194320 | tf_op jit(solution)/shard_map/all_gather | solution.py:32
  114.8 1.5 broadcast.67.clone.1
  116.3 1.5 broadcast.67.clone
  117.8 1.5 broadcast.67
  119.3 135.4 %while.28 = (s32[]{:T(128)}, bf16[32,8192]{1,0:T(8,128)(2,1)S(1)}, bf16[128,8192]{1,0:T(8,128)(2,1)}, bf16[128,8192]{1,0:T(8,128)(2,1)}, bf16[128,256]{1,0:T(8,1...) while((s32[]{:T(128)}, bf16[32,8192]{1,0:T(8,128)(2,1)S(1)}, ...), condition=%wide.region_4.5_spmd.clone, body=%wide.region_0.4_spmd.clone.sunk | while | flops 546234496 | bytes 63868848 | solution.py:91
  119.7 3.2 select_dynamic-update-slice_fusion.8
  123.1 2.4 fusion.48
  126.4 1.3 copy-done
  127.7 1.5 fusion.49
  129.2 3.0 select_dynamic-update-slice_fusion.10
  132.2 1.3 collective-permute-start
  133.5 14.7 %collective-permute-done = bf16[32,8192]{1,0:T(8,128)(2,1)S(1)} collective-permute-done((bf16[32,8192]{1,0:T(8,128)(2,1)S(1)}, bf16[32,8192]{1,0:T(8,128)(2,1)S(1)}, u32[]{:S(2)}, u32[]{:S(2)}) %collective-permute-start) | collective-permute-done | bytes 524320 | tf_op jit(solution)/shard_map/while/body/eval_jaxpr/ppermute | solution.py:15
  148.5 3.2 select_dynamic-update-slice_fusion.8
  152.0 2.4 fusion.48
  155.2 1.3 copy-done
  156.6 1.5 fusion.49
  158.1 3.0 select_dynamic-update-slice_fusion.10
  161.1 1.3 collective-permute-start
  162.4 13.8 %collective-permute-done = bf16[32,8192]{1,0:T(8,128)(2,1)S(1)} collective-permute-done((bf16[32,8192]{1,0:T(8,128)(2,1)S(1)}, bf16[32,8192]{1,0:T(8,128)(2,1)S(1)}, u32[]{:S(2)}, u32[]{:S(2)}) %collective-permute-start) | collective-permute-done | bytes 524320 | tf_op jit(solution)/shard_map/while/body/eval_jaxpr/ppermute | solution.py:15
  176.6 3.2 select_dynamic-update-slice_fusion.8
  180.0 2.4 fusion.48
  183.3 1.3 copy-done
  184.6 1.5 fusion.49
  186.1 3.0 select_dynamic-update-slice_fusion.10
  189.1 1.3 collective-permute-start
  190.4 12.9 %collective-permute-done = bf16[32,8192]{1,0:T(8,128)(2,1)S(1)} collective-permute-done((bf16[32,8192]{1,0:T(8,128)(2,1)S(1)}, bf16[32,8192]{1,0:T(8,128)(2,1)S(1)}, u32[]{:S(2)}, u32[]{:S(2)}) %collective-permute-start) | collective-permute-done | bytes 524320 | tf_op jit(solution)/shard_map/while/body/eval_jaxpr/ppermute | solution.py:15
  203.7 3.2 select_dynamic-update-slice_fusion.8
  207.1 2.4 fusion.48
  210.4 1.3 copy-done
  211.7 1.5 fusion.49
  213.2 3.0 select_dynamic-update-slice_fusion.10
  216.2 1.3 collective-permute-start
  217.5 12.0 %collective-permute-done = bf16[32,8192]{1,0:T(8,128)(2,1)S(1)} collective-permute-done((bf16[32,8192]{1,0:T(8,128)(2,1)S(1)}, bf16[32,8192]{1,0:T(8,128)(2,1)S(1)}, u32[]{:S(2)}, u32[]{:S(2)}) %collective-permute-start) | collective-permute-done | bytes 524320 | tf_op jit(solution)/shard_map/while/body/eval_jaxpr/ppermute | solution.py:15
  229.8 3.2 select_dynamic-update-slice_fusion.8
  233.3 2.4 fusion.48
  236.5 1.3 copy-done
  237.9 1.5 fusion.49
  239.3 3.0 select_dynamic-update-slice_fusion.10
  242.4 1.3 collective-permute-start
  243.7 11.1 %collective-permute-done = bf16[32,8192]{1,0:T(8,128)(2,1)S(1)} collective-permute-done((bf16[32,8192]{1,0:T(8,128)(2,1)S(1)}, bf16[32,8192]{1,0:T(8,128)(2,1)S(1)}, u32[]{:S(2)}, u32[]{:S(2)}) %collective-permute-start) | collective-permute-done | bytes 524320 | tf_op jit(solution)/shard_map/while/body/eval_jaxpr/ppermute | solution.py:15
  254.8 5.0 %convolution_convert_fusion.1 = bf16[8192,256]{0,1:T(8,128)(2,1)} fusion(bf16[128,8192]{1,0:T(8,128)(2,1)} %get-tuple-element.369, bf16[128,256]{1,0:T(8,128)(2,1)S(1)} %get-tuple-element.370), kind=kOutput, calls=%fused_computation.36 | convolution fusion | flops 538968064 | bytes 6356992 | tf_op jit(solution)/shard_map/td,tr->dr/dot_general | solution.py:93
  259.7 3.2 convolution_convert_fusion
  263.0 7.7 %pad_maximum_fusion = bf16[8192,512]{0,1:T(8,128)(2,1)} fusion(bf16[8192,256]{0,1:T(8,128)(2,1)} %convolution_convert_fusion, bf16[8192,256]{0,1:T(8,128)(2,1)} %convolution_convert_fusion.1), kind=kLoop, calls=%fused_computation.37 | loop fusion | flops 16777216 | bytes 16777216 | tf_op jit(solution)/shard_map/concatenate | solution.py:96
  272.5 59.9 %all-reduce = f32[8192]{0:T(1024)S(1)} all-reduce(f32[8192]{0:T(1024)S(1)} %get-tuple-element.373), channel_id=5, replica_groups=mesh['section'=2,'dp'=16] {'dp'}, use_global_device_ids=true, to_apply=%region_6.7.clone | all-reduce | flops 8192 | bytes 65536
  333.1 40.4 %reduce-scatter.2.cloned.1.call-done = bf16[512,512]{0,1:T(8,128)(2,1)} async-done(((bf16[8192,512]{0,1:T(8,128)(2,1)}), bf16[512,512]{0,1:T(8,128)(2,1)}) %reduce-scatter.2.cloned.1.call-update) | async-done | bytes 524304 | tf_op jit(solution)/shard_map/reduce_scatter | solution.py:95
  373.5 1.2 convert_multiply_fusion.3
  374.8 1.0 copy.13
  (69 shorter events, 11.4 us)
Async XLA Ops:
  7.2 56.3 %all-gather.5.cloned.1.call-start = ((), (), s32[]{:S(2)}) async-start(), calls=%async_computation.2 | async-start | bytes 4456448 | tf_op jit(solution)/shard_map/all_gather | solution.py:31
  7.9 106.8 %all-gather.7.cloned.1.call-start = ((), (), s32[]{:S(2)}) async-start(), calls=%async_computation.3 | async-start | bytes 4456448 | tf_op jit(solution)/shard_map/all_gather | solution.py:32
  8.6 364.9 %reduce-scatter.2.cloned.1.call-start = ((), (), s32[]{:S(2)}) async-start(), calls=%async_computation.1 | async-start | bytes 8912896 | tf_op jit(solution)/shard_map/reduce_scatter | solution.py:95
  116.3 3.0 copy-start.2
  116.3 3.0 copy-start.4
  116.3 3.0 copy-start.5
  119.7 3.5 copy-start.1
  125.6 2.2 copy-start
  132.2 16.0 %collective-permute-start = (bf16[32,8192]{1,0:T(8,128)(2,1)S(1)}, bf16[32,8192]{1,0:T(8,128)(2,1)S(1)}, u32[]{:S(2)}, u32[]{:S(2)}) collective-permute-start(bf16[32,8192]{1,0:T(8,128)(2,1)S(1)} %get-tuple-element.590), channel_id=1, source_target_pairs={{16,0},{17,1},{18,2},{19,3},{20,4},{21,5},{22,6},{23,7},{24,8},{25... | collective-permute-start | bytes 1572872 | tf_op jit(solution)/shard_map/while/body/eval_jaxpr/ppermute | solution.py:15
  148.5 3.5 copy-start.1
  154.4 2.2 copy-start
  161.1 15.2 %collective-permute-start = (bf16[32,8192]{1,0:T(8,128)(2,1)S(1)}, bf16[32,8192]{1,0:T(8,128)(2,1)S(1)}, u32[]{:S(2)}, u32[]{:S(2)}) collective-permute-start(bf16[32,8192]{1,0:T(8,128)(2,1)S(1)} %get-tuple-element.590), channel_id=1, source_target_pairs={{16,0},{17,1},{18,2},{19,3},{20,4},{21,5},{22,6},{23,7},{24,8},{25... | collective-permute-start | bytes 1572872 | tf_op jit(solution)/shard_map/while/body/eval_jaxpr/ppermute | solution.py:15
  176.5 3.5 copy-start.1
  182.4 2.2 copy-start
  189.1 14.2 %collective-permute-start = (bf16[32,8192]{1,0:T(8,128)(2,1)S(1)}, bf16[32,8192]{1,0:T(8,128)(2,1)S(1)}, u32[]{:S(2)}, u32[]{:S(2)}) collective-permute-start(bf16[32,8192]{1,0:T(8,128)(2,1)S(1)} %get-tuple-element.590), channel_id=1, source_target_pairs={{16,0},{17,1},{18,2},{19,3},{20,4},{21,5},{22,6},{23,7},{24,8},{25... | collective-permute-start | bytes 1572872 | tf_op jit(solution)/shard_map/while/body/eval_jaxpr/ppermute | solution.py:15
  203.6 3.5 copy-start.1
  209.5 2.2 copy-start
  216.2 13.3 %collective-permute-start = (bf16[32,8192]{1,0:T(8,128)(2,1)S(1)}, bf16[32,8192]{1,0:T(8,128)(2,1)S(1)}, u32[]{:S(2)}, u32[]{:S(2)}) collective-permute-start(bf16[32,8192]{1,0:T(8,128)(2,1)S(1)} %get-tuple-element.590), channel_id=1, source_target_pairs={{16,0},{17,1},{18,2},{19,3},{20,4},{21,5},{22,6},{23,7},{24,8},{25... | collective-permute-start | bytes 1572872 | tf_op jit(solution)/shard_map/while/body/eval_jaxpr/ppermute | solution.py:15
  229.8 3.5 copy-start.1
  235.7 2.2 copy-start
  242.4 12.4 %collective-permute-start = (bf16[32,8192]{1,0:T(8,128)(2,1)S(1)}, bf16[32,8192]{1,0:T(8,128)(2,1)S(1)}, u32[]{:S(2)}, u32[]{:S(2)}) collective-permute-start(bf16[32,8192]{1,0:T(8,128)(2,1)S(1)} %get-tuple-element.590), channel_id=1, source_target_pairs={{16,0},{17,1},{18,2},{19,3},{20,4},{21,5},{22,6},{23,7},{24,8},{25... | collective-permute-start | bytes 1572872 | tf_op jit(solution)/shard_map/while/body/eval_jaxpr/ppermute | solution.py:15
  254.8 5.0 %copy-start.3 = (bf16[128,8192]{1,0:T(8,128)(2,1)S(1)}, bf16[128,8192]{1,0:T(8,128)(2,1)}, u32[]{:S(2)}) copy-start(bf16[128,8192]{1,0:T(8,128)(2,1)} %get-tuple-element.371) | copy-start | bytes 6291460
  270.7 0.7 copy-start.6
Sparse Core Ops, SparseCore 0:
  10.2 53.2 all-gather.4
  65.6 49.0 all-gather.6
  270.8 102.6 reduce-scatter.1
where the time goes:
time: 384 us; the launch traced here: 383 us
  waiting for transfers between devices  212 us (55%)
  blocking collectives  59.9 us (16%)
  matrix products  47.9 us (12%)
  other arithmetic  26.3 us (7%)
  local copies, waits for them, and re-layouts  15.7 us (4%)
  between operations  14.5 us (4%)
  starting transfers between devices  6.52 us (2%)
    ppermute x5, waiting for transfers between devices, shifted(): return lax.ppermute(block, axis, route)  64.5 us
    unnamed x1, blocking collectives  59.9 us
    all_gather x1, waiting for transfers between devices, local(): lax.all_gather(w_down[0], 'dp', axis=0, tiled=True)  54.7 us
    all_gather x1, waiting for transfers between devices, local(): lax.all_gather(w_up[0], 'dp', axis=0, tiled=True)  51.2 us
    reduce_scatter x1, waiting for transfers between devices, local(): lax.psum_scatter(jnp.concatenate([down_part, up_part], axis=1).astype(jnp...  40.4 us
    dot_general x5, matrix products, run_step(): preact = jnp.dot(scaled, down_matrix, preferred_element_type=jnp.float32)  16.2 us
    dynamic_update_slice x5, other arithmetic, write_rows(): lax.dynamic_update_slice_in_dim(buffer, jnp.where(active_step, fresh, pre...  15.1 us
    dot_general x5, matrix products, run_step(): jnp.einsum('tr,dr->td', hidden, up_matrix, preferred_element_type=jnp.flo...  12 us
  transfers between devices with their start and end apart: 8, of which 8 were waited for; matrix products, arithmetic and copies ran while one was open for 0% of the time, Pallas kernels for 0%

commit v1 on v0

--- a/solution.py
+++ b/solution.py
@@ -7,6 +7,28 @@
 ROWS = 32
 TOK_DEV = 128
 EPSILON = 1e-05
+
+
+def joined_along(blocks, dim):
+    shape = list(blocks.shape[1:])
+    shape[dim] *= blocks.shape[0]
+    return jnp.moveaxis(blocks, 0, dim).reshape(shape)
+
+
+def gather_around(x, axis, dim):
+    size = lax.axis_size(axis)
+    pairs = [(i, (i + 1) % size) for i in range(size)]
+    back = [(b, a) for a, b in pairs]
+    lower, upper = ([], [])
+    for step in range(size - 1):
+        if step % 2 == 0:
+            lower.append(lax.ppermute(lower[-1] if lower else x, axis, pairs))
+        else:
+            upper.append(lax.ppermute(upper[-1] if upper else x, axis, back))
+    pieces = jnp.stack([*lower[::-1], x, *upper])
+    shift = lax.axis_index(axis) - len(lower)
+    pieces = pieces[(jnp.arange(size) - shift) % size]
+    return joined_along(pieces, dim)
 
 
 def shifted(block, axis, distance):
@@ -28,7 +50,7 @@
     layer_inputs = section_inputs[0]
     gain = gains[0]
     down_matrix, up_matrix = (
-        lax.all_gather(w_down[0], "dp", axis=0, tiled=True),
+        gather_around(w_down[0], "dp", 0),
         lax.all_gather(w_up[0], "dp", axis=0, tiled=True),
     )
     is_last = section_index == sections - 1

time: 384 us -> 370 us (0.964)
  waiting for transfers between devices: 212 us -> 140 us
  starting transfers between devices: 6.52 us -> 39.3 us
  blocking collectives: 59.9 us -> 72.4 us
  local copies, waits for them, and re-layouts: 15.7 us -> 27.4 us
    all_gather x1 -> x0, waiting for transfers between devices: 54.7 us -> none  [local(): lax.all_gather(w_down[0], 'dp', axis=0, tiled=True)]
    all_gather x1, waiting for transfers between devices: 51.2 us -> 0.01 us  [local(): lax.all_gather(w_up[0], 'dp', axis=0, tiled=True)]
    ppermute x0 -> x15, waiting for transfers between devices: none -> 46.3 us  [the longest x8 28.4 us: gather_around(): lower.append(lax.ppermute(lower[-1] if lower else x, axis, pairs))]
    ppermute x0 -> x15, starting transfers between devices: none -> 32.8 us  [the longest x7 32.3 us: gather_around(): upper.append(lax.ppermute(upper[-1] if upper else x, axis, back))]
    ppermute x5, waiting for transfers between devices: 64.5 us -> 48.8 us  [shifted(): return lax.ppermute(block, axis, route)]
    unnamed x13 -> x30, local copies, waits for them, and re-layouts: 3.21 us -> 15.9 us
    unnamed x1, blocking collectives: 59.9 us -> 72.4 us
    while x20, local copies, waits for them, and re-layouts: 7.77 us -> 1.11 us
  transfers between devices with their start and end apart: 8 -> 22, of which waited for: 8 -> 20; matrix products, arithmetic and copies ran while one was open for 0% -> 5% of each run, Pallas kernels for 0% -> 0%
where the time goes in v1:
time: 370 us
  waiting for transfers between devices  140 us (38%)
  blocking collectives  72.4 us (20%)
  matrix products  48.6 us (13%)
  starting transfers between devices  39.3 us (11%)
  local copies, waits for them, and re-layouts  27.4 us (7%)
  other arithmetic  26.3 us (7%)
  between operations  14.8 us (4%)
    unnamed x1, blocking collectives  72.4 us
    ppermute x5, waiting for transfers between devices, shifted(): return lax.ppermute(block, axis, route)  48.8 us
    reduce_scatter x1, waiting for transfers between devices, local(): lax.psum_scatter(jnp.concatenate([down_part, up_part], axis=1).astype(jnp...  44.7 us
    ppermute x7, starting transfers between devices, gather_around(): upper.append(lax.ppermute(upper[-1] if upper else x, axis, back))  32.3 us
    ppermute x8, waiting for transfers between devices, gather_around(): lower.append(lax.ppermute(lower[-1] if lower else x, axis, pairs))  28.4 us
    ppermute x7, waiting for transfers between devices, gather_around(): upper.append(lax.ppermute(upper[-1] if upper else x, axis, back))  17.9 us
    dot_general x5, matrix products, run_step(): preact = jnp.dot(scaled, down_matrix, preferred_element_type=jnp.float32)  16.1 us
    unnamed x30, local copies, waits for them, and re-layouts  15.9 us
  transfers between devices with their start and end apart: 22, of which 20 were waited for; matrix products, arithmetic and copies ran while one was open for 5% of the time, Pallas kernels for 0%

profile of v1, /device:TPU:0, one launch (start us, length us, event | category | flops | bytes accessed | tf_op | source)
XLA Modules:
  0.0 369.7 jit_solution(1765230415330807652)
XLA Ops:
  8.5 9.3 %collective-permute-done.1 = bf16[512,256]{1,0:T(8,128)(2,1)S(1)} collective-permute-done((bf16[512,256]{1,0:T(8,128)(2,1)}, bf16[512,256]{1,0:T(8,128)(2,1)S(1)}, u32[]{:S(2)}, u32[]{:S(2)}) %collective-permute-start.1) | collective-permute-done | bytes 262176 | tf_op jit(solution)/shard_map/ppermute | solution.py:25
  17.7 4.4 %collective-permute-start.9 = (bf16[512,256]{1,0:T(8,128)(2,1)}, bf16[512,256]{1,0:T(8,128)(2,1)S(1)}, u32[]{:S(2)}, u32[]{:S(2)}) collective-permute-start(bf16[512,256]{1,0:T(8,128)(2,1)} %bitcast.76), channel_id=1, source_target_pairs={{1,0},{2,1},{3,2},{4,3},{5,4},{6,5},{7,6},{8,7},{9,8},{10,9},{11,1... | collective-permute-start | bytes 786440 | tf_op jit(solution)/shard_map/ppermute | solution.py:27
  22.2 4.3 %collective-permute-done.2 = bf16[512,256]{1,0:T(8,128)(2,1)S(1)} collective-permute-done((bf16[512,256]{1,0:T(8,128)(2,1)S(1)}, bf16[512,256]{1,0:T(8,128)(2,1)S(1)}, u32[]{:S(2)}, u32[]{:S(2)}) %collective-permute-start.2) | collective-permute-done | bytes 262176 | tf_op jit(solution)/shard_map/ppermute | solution.py:25
  27.3 4.6 %collective-permute-start.10 = (bf16[512,256]{1,0:T(8,128)(2,1)S(1)}, bf16[512,256]{1,0:T(8,128)(2,1)S(1)}, u32[]{:S(2)}, u32[]{:S(2)}) collective-permute-start(bf16[512,256]{1,0:T(8,128)(2,1)S(1)} %collective-permute-done.9), channel_id=1, source_target_pairs={{1,0},{2,1},{3,2},{4,3},{5,4},{6,5},{7,6},{8,7},{9,8},{10,9},{11,1... | collective-permute-start | bytes 786440 | tf_op jit(solution)/shard_map/ppermute | solution.py:27
  31.9 4.5 %collective-permute-done.3 = bf16[512,256]{1,0:T(8,128)(2,1)S(1)} collective-permute-done((bf16[512,256]{1,0:T(8,128)(2,1)S(1)}, bf16[512,256]{1,0:T(8,128)(2,1)S(1)}, u32[]{:S(2)}, u32[]{:S(2)}) %collective-permute-start.3) | collective-permute-done | bytes 262176 | tf_op jit(solution)/shard_map/ppermute | solution.py:25
  37.5 4.7 %collective-permute-start.11 = (bf16[512,256]{1,0:T(8,128)(2,1)S(1)}, bf16[512,256]{1,0:T(8,128)(2,1)S(1)}, u32[]{:S(2)}, u32[]{:S(2)}) collective-permute-start(bf16[512,256]{1,0:T(8,128)(2,1)S(1)} %collective-permute-done.10), channel_id=1, source_target_pairs={{1,0},{2,1},{3,2},{4,3},{5,4},{6,5},{7,6},{8,7},{9,8},{10,9},{11,1... | collective-permute-start | bytes 786440 | tf_op jit(solution)/shard_map/ppermute | solution.py:27
  42.2 2.7 collective-permute-done.4
  44.9 6.1 %collective-permute-done.11 = bf16[512,256]{1,0:T(8,128)(2,1)S(1)} collective-permute-done((bf16[512,256]{1,0:T(8,128)(2,1)S(1)}, bf16[512,256]{1,0:T(8,128)(2,1)S(1)}, u32[]{:S(2)}, u32[]{:S(2)}) %collective-permute-start.11) | collective-permute-done | bytes 262176 | tf_op jit(solution)/shard_map/ppermute | solution.py:27
  51.0 4.6 %collective-permute-start.12 = (bf16[512,256]{1,0:T(8,128)(2,1)S(1)}, bf16[512,256]{1,0:T(8,128)(2,1)S(1)}, u32[]{:S(2)}, u32[]{:S(2)}) collective-permute-start(bf16[512,256]{1,0:T(8,128)(2,1)S(1)} %collective-permute-done.11), channel_id=1, source_target_pairs={{1,0},{2,1},{3,2},{4,3},{5,4},{6,5},{7,6},{8,7},{9,8},{10,9},{11,1... | collective-permute-start | bytes 786440 | tf_op jit(solution)/shard_map/ppermute | solution.py:27
  55.6 3.4 collective-permute-done.5
  59.7 4.7 %collective-permute-start.13 = (bf16[512,256]{1,0:T(8,128)(2,1)S(1)}, bf16[512,256]{1,0:T(8,128)(2,1)S(1)}, u32[]{:S(2)}, u32[]{:S(2)}) collective-permute-start(bf16[512,256]{1,0:T(8,128)(2,1)S(1)} %collective-permute-done.12), channel_id=1, source_target_pairs={{1,0},{2,1},{3,2},{4,3},{5,4},{6,5},{7,6},{8,7},{9,8},{10,9},{11,1... | collective-permute-start | bytes 786440 | tf_op jit(solution)/shard_map/ppermute | solution.py:27
  64.4 3.3 collective-permute-done.6
  67.6 5.6 %collective-permute-done.13 = bf16[512,256]{1,0:T(8,128)(2,1)S(1)} collective-permute-done((bf16[512,256]{1,0:T(8,128)(2,1)S(1)}, bf16[512,256]{1,0:T(8,128)(2,1)S(1)}, u32[]{:S(2)}, u32[]{:S(2)}) %collective-permute-start.13) | collective-permute-done | bytes 262176 | tf_op jit(solution)/shard_map/ppermute | solution.py:27
  73.3 4.6 %collective-permute-start.14 = (bf16[512,256]{1,0:T(8,128)(2,1)S(1)}, bf16[512,256]{1,0:T(8,128)(2,1)S(1)}, u32[]{:S(2)}, u32[]{:S(2)}) collective-permute-start(bf16[512,256]{1,0:T(8,128)(2,1)S(1)} %collective-permute-done.13), channel_id=1, source_target_pairs={{1,0},{2,1},{3,2},{4,3},{5,4},{6,5},{7,6},{8,7},{9,8},{10,9},{11,1... | collective-permute-start | bytes 786440 | tf_op jit(solution)/shard_map/ppermute | solution.py:27
  78.4 3.4 collective-permute-done.14
  81.8 4.7 %collective-permute-start.15 = (bf16[512,256]{1,0:T(8,128)(2,1)S(1)}, bf16[512,256]{1,0:T(8,128)(2,1)S(1)}, u32[]{:S(2)}, u32[]{:S(2)}) collective-permute-start(bf16[512,256]{1,0:T(8,128)(2,1)S(1)} %collective-permute-done.14), channel_id=1, source_target_pairs={{1,0},{2,1},{3,2},{4,3},{5,4},{6,5},{7,6},{8,7},{9,8},{10,9},{11,1... | collective-permute-start | bytes 786440 | tf_op jit(solution)/shard_map/ppermute | solution.py:27
  87.1 1.7 bitcast_dynamic-update-slice_fusion.14
  88.8 1.7 bitcast_dynamic-update-slice_fusion.13
  100.5 5.0 %gather_fusion = bf16[16,512,256]{2,1,0:T(8,128)(2,1)} fusion(bf16[16,512,256]{2,1,0:T(8,128)(2,1)} %bitcast_dynamic-update-slice_fusion, s32[1024]{0:T(1024)S(1)} %pad_clamp_fusion), kind=kCustom, calls=%fused_computation | custom fusion | bytes 8388672 | tf_op jit(solution)/shard_map/gather | solution.py:30
  105.6 1.5 broadcast.130
  107.1 1.5 broadcast.130.clone
  108.6 1.5 broadcast.130.clone.1
  110.3 113.8 %while.28 = (s32[]{:T(128)}, bf16[32,8192]{1,0:T(8,128)(2,1)S(1)}, bf16[128,8192]{1,0:T(8,128)(2,1)}, bf16[128,8192]{1,0:T(8,128)(2,1)}, bf16[128,256]{1,0:T(8,1...) while((s32[]{:T(128)}, bf16[32,8192]{1,0:T(8,128)(2,1)S(1)}, ...), condition=%wide.region_4.5_spmd.clone, body=%wide.region_0.4_spmd.clone.sunk | while | flops 546234496 | bytes 63868848 | solution.py:113
  110.6 3.2 select_dynamic-update-slice_fusion.8
  114.1 2.6 fusion.50
  119.0 3.0 select_dynamic-update-slice_fusion.10
  123.3 9.8 %collective-permute-done = bf16[32,8192]{1,0:T(8,128)(2,1)S(1)} collective-permute-done((bf16[32,8192]{1,0:T(8,128)(2,1)S(1)}, bf16[32,8192]{1,0:T(8,128)(2,1)S(1)}, u32[]{:S(2)}, u32[]{:S(2)}) %collective-permute-start) | collective-permute-done | bytes 524320 | tf_op jit(solution)/shard_map/while/body/eval_jaxpr/ppermute | solution.py:37
  133.4 3.2 select_dynamic-update-slice_fusion.8
  136.8 2.6 fusion.50
  141.7 3.0 select_dynamic-update-slice_fusion.10
  146.0 9.8 %collective-permute-done = bf16[32,8192]{1,0:T(8,128)(2,1)S(1)} collective-permute-done((bf16[32,8192]{1,0:T(8,128)(2,1)S(1)}, bf16[32,8192]{1,0:T(8,128)(2,1)S(1)}, u32[]{:S(2)}, u32[]{:S(2)}) %collective-permute-start) | collective-permute-done | bytes 524320 | tf_op jit(solution)/shard_map/while/body/eval_jaxpr/ppermute | solution.py:37
  156.1 3.2 select_dynamic-update-slice_fusion.8
  159.6 2.6 fusion.50
  164.4 3.0 select_dynamic-update-slice_fusion.10
  168.8 9.8 %collective-permute-done = bf16[32,8192]{1,0:T(8,128)(2,1)S(1)} collective-permute-done((bf16[32,8192]{1,0:T(8,128)(2,1)S(1)}, bf16[32,8192]{1,0:T(8,128)(2,1)S(1)}, u32[]{:S(2)}, u32[]{:S(2)}) %collective-permute-start) | collective-permute-done | bytes 524320 | tf_op jit(solution)/shard_map/while/body/eval_jaxpr/ppermute | solution.py:37
  178.9 3.2 select_dynamic-update-slice_fusion.8
  182.3 2.6 fusion.50
  187.2 3.0 select_dynamic-update-slice_fusion.10
  191.5 9.8 %collective-permute-done = bf16[32,8192]{1,0:T(8,128)(2,1)S(1)} collective-permute-done((bf16[32,8192]{1,0:T(8,128)(2,1)S(1)}, bf16[32,8192]{1,0:T(8,128)(2,1)S(1)}, u32[]{:S(2)}, u32[]{:S(2)}) %collective-permute-start) | collective-permute-done | bytes 524320 | tf_op jit(solution)/shard_map/while/body/eval_jaxpr/ppermute | solution.py:37
  201.6 3.2 select_dynamic-update-slice_fusion.8
  205.1 2.6 fusion.50
  209.9 3.0 select_dynamic-update-slice_fusion.10
  214.3 9.8 %collective-permute-done = bf16[32,8192]{1,0:T(8,128)(2,1)S(1)} collective-permute-done((bf16[32,8192]{1,0:T(8,128)(2,1)S(1)}, bf16[32,8192]{1,0:T(8,128)(2,1)S(1)}, u32[]{:S(2)}, u32[]{:S(2)}) %collective-permute-start) | collective-permute-done | bytes 524320 | tf_op jit(solution)/shard_map/while/body/eval_jaxpr/ppermute | solution.py:37
  224.0 5.0 %convolution_convert_fusion.1 = bf16[8192,256]{0,1:T(8,128)(2,1)} fusion(bf16[128,8192]{1,0:T(8,128)(2,1)} %get-tuple-element.369, bf16[128,256]{1,0:T(8,128)(2,1)S(1)} %get-tuple-element.370), kind=kOutput, calls=%fused_computation.37 | convolution fusion | flops 538968064 | bytes 6356992 | tf_op jit(solution)/shard_map/td,tr->dr/dot_general | solution.py:115
  229.0 3.2 convolution_convert_fusion
  232.3 7.7 %pad_maximum_fusion = bf16[8192,512]{0,1:T(8,128)(2,1)} fusion(bf16[8192,256]{0,1:T(8,128)(2,1)} %convolution_convert_fusion, bf16[8192,256]{0,1:T(8,128)(2,1)} %convolution_convert_fusion.1), kind=kLoop, calls=%fused_computation.38 | loop fusion | flops 16777216 | bytes 16777216 | tf_op jit(solution)/shard_map/concatenate | solution.py:118
  241.9 72.4 %all-reduce = f32[8192]{0:T(1024)S(1)} all-reduce(f32[8192]{0:T(1024)S(1)} %get-tuple-element.373), channel_id=4, replica_groups=mesh['section'=2,'dp'=16] {'dp'}, use_global_device_ids=true, to_apply=%region_6.7.clone | all-reduce | flops 8192 | bytes 65536
  314.9 44.7 %reduce-scatter.2.cloned.1.call-done = bf16[512,512]{0,1:T(8,128)(2,1)} async-done(((bf16[8192,512]{0,1:T(8,128)(2,1)}), bf16[512,512]{0,1:T(8,128)(2,1)}) %reduce-scatter.2.cloned.1.call-update) | async-done | bytes 524304 | tf_op jit(solution)/shard_map/reduce_scatter | solution.py:117
  (117 shorter events, 41.1 us)
Async XLA Ops:
  7.2 87.6 %copy-start.5 = (bf16[1,512,256]{2,1,0:T(8,128)(2,1)S(1)}, bf16[1,512,256]{2,1,0:T(8,128)(2,1)}, u32[]{:S(2)}) copy-start(bf16[1,512,256]{2,1,0:T(8,128)(2,1)} %param.12) | copy-start | bytes 786436
  7.2 98.4 %all-gather.3.cloned.1.call-start = ((), (), s32[]{:S(2)}) async-start(), calls=%async_computation.2 | async-start | bytes 4456448 | tf_op jit(solution)/shard_map/all_gather | solution.py:54
  7.9 351.7 %reduce-scatter.2.cloned.1.call-start = ((), (), s32[]{:S(2)}) async-start(), calls=%async_computation.1 | async-start | bytes 8912896 | tf_op jit(solution)/shard_map/reduce_scatter | solution.py:117
  8.0 9.8 %collective-permute-start.1 = (bf16[512,256]{1,0:T(8,128)(2,1)}, bf16[512,256]{1,0:T(8,128)(2,1)S(1)}, u32[]{:S(2)}, u32[]{:S(2)}) collective-permute-start(bf16[512,256]{1,0:T(8,128)(2,1)} %bitcast.75), channel_id=1, source_target_pairs={{0,1},{1,2},{2,3},{3,4},{4,5},{5,6},{6,7},{7,8},{8,9},{9,10},{10,1... | collective-permute-start | bytes 786440 | tf_op jit(solution)/shard_map/ppermute | solution.py:25
  17.7 8.7 %collective-permute-start.2 = (bf16[512,256]{1,0:T(8,128)(2,1)S(1)}, bf16[512,256]{1,0:T(8,128)(2,1)S(1)}, u32[]{:S(2)}, u32[]{:S(2)}) collective-permute-start(bf16[512,256]{1,0:T(8,128)(2,1)S(1)} %collective-permute-done.1), channel_id=1, source_target_pairs={{0,1},{1,2},{2,3},{3,4},{4,5},{5,6},{6,7},{7,8},{8,9},{9,10},{10,1... | collective-permute-start | bytes 786440 | tf_op jit(solution)/shard_map/ppermute | solution.py:25
  17.7 9.5 %collective-permute-start.9 = (bf16[512,256]{1,0:T(8,128)(2,1)}, bf16[512,256]{1,0:T(8,128)(2,1)S(1)}, u32[]{:S(2)}, u32[]{:S(2)}) collective-permute-start(bf16[512,256]{1,0:T(8,128)(2,1)} %bitcast.76), channel_id=1, source_target_pairs={{1,0},{2,1},{3,2},{4,3},{5,4},{6,5},{7,6},{8,7},{9,8},{10,9},{11,1... | collective-permute-start | bytes 786440 | tf_op jit(solution)/shard_map/ppermute | solution.py:27
  26.4 9.9 %collective-permute-start.3 = (bf16[512,256]{1,0:T(8,128)(2,1)S(1)}, bf16[512,256]{1,0:T(8,128)(2,1)S(1)}, u32[]{:S(2)}, u32[]{:S(2)}) collective-permute-start(bf16[512,256]{1,0:T(8,128)(2,1)S(1)} %collective-permute-done.2), channel_id=1, source_target_pairs={{0,1},{1,2},{2,3},{3,4},{4,5},{5,6},{6,7},{7,8},{8,9},{9,10},{10,1... | collective-permute-start | bytes 786440 | tf_op jit(solution)/shard_map/ppermute | solution.py:25
  27.3 10.3 %collective-permute-start.10 = (bf16[512,256]{1,0:T(8,128)(2,1)S(1)}, bf16[512,256]{1,0:T(8,128)(2,1)S(1)}, u32[]{:S(2)}, u32[]{:S(2)}) collective-permute-start(bf16[512,256]{1,0:T(8,128)(2,1)S(1)} %collective-permute-done.9), channel_id=1, source_target_pairs={{1,0},{2,1},{3,2},{4,3},{5,4},{6,5},{7,6},{8,7},{9,8},{10,9},{11,1... | collective-permute-start | bytes 786440 | tf_op jit(solution)/shard_map/ppermute | solution.py:27
  36.3 8.6 %collective-permute-start.4 = (bf16[512,256]{1,0:T(8,128)(2,1)S(1)}, bf16[512,256]{1,0:T(8,128)(2,1)S(1)}, u32[]{:S(2)}, u32[]{:S(2)}) collective-permute-start(bf16[512,256]{1,0:T(8,128)(2,1)S(1)} %collective-permute-done.3), channel_id=1, source_target_pairs={{0,1},{1,2},{2,3},{3,4},{4,5},{5,6},{6,7},{7,8},{8,9},{9,10},{10,1... | collective-permute-start | bytes 786440 | tf_op jit(solution)/shard_map/ppermute | solution.py:25
  37.5 13.4 %collective-permute-start.11 = (bf16[512,256]{1,0:T(8,128)(2,1)S(1)}, bf16[512,256]{1,0:T(8,128)(2,1)S(1)}, u32[]{:S(2)}, u32[]{:S(2)}) collective-permute-start(bf16[512,256]{1,0:T(8,128)(2,1)S(1)} %collective-permute-done.10), channel_id=1, source_target_pairs={{1,0},{2,1},{3,2},{4,3},{5,4},{6,5},{7,6},{8,7},{9,8},{10,9},{11,1... | collective-permute-start | bytes 786440 | tf_op jit(solution)/shard_map/ppermute | solution.py:27
  44.9 14.1 %collective-permute-start.5 = (bf16[512,256]{1,0:T(8,128)(2,1)S(1)}, bf16[512,256]{1,0:T(8,128)(2,1)S(1)}, u32[]{:S(2)}, u32[]{:S(2)}) collective-permute-start(bf16[512,256]{1,0:T(8,128)(2,1)S(1)} %collective-permute-done.4), channel_id=1, source_target_pairs={{0,1},{1,2},{2,3},{3,4},{4,5},{5,6},{6,7},{7,8},{8,9},{9,10},{10,1... | collective-permute-start | bytes 786440 | tf_op jit(solution)/shard_map/ppermute | solution.py:25
  51.0 8.7 %collective-permute-start.12 = (bf16[512,256]{1,0:T(8,128)(2,1)S(1)}, bf16[512,256]{1,0:T(8,128)(2,1)S(1)}, u32[]{:S(2)}, u32[]{:S(2)}) collective-permute-start(bf16[512,256]{1,0:T(8,128)(2,1)S(1)} %collective-permute-done.11), channel_id=1, source_target_pairs={{1,0},{2,1},{3,2},{4,3},{5,4},{6,5},{7,6},{8,7},{9,8},{10,9},{11,1... | collective-permute-start | bytes 786440 | tf_op jit(solution)/shard_map/ppermute | solution.py:27
  59.0 8.6 %collective-permute-start.6 = (bf16[512,256]{1,0:T(8,128)(2,1)S(1)}, bf16[512,256]{1,0:T(8,128)(2,1)S(1)}, u32[]{:S(2)}, u32[]{:S(2)}) collective-permute-start(bf16[512,256]{1,0:T(8,128)(2,1)S(1)} %collective-permute-done.5), channel_id=1, source_target_pairs={{0,1},{1,2},{2,3},{3,4},{4,5},{5,6},{6,7},{7,8},{8,9},{9,10},{10,1... | collective-permute-start | bytes 786440 | tf_op jit(solution)/shard_map/ppermute | solution.py:25
  59.7 13.6 %collective-permute-start.13 = (bf16[512,256]{1,0:T(8,128)(2,1)S(1)}, bf16[512,256]{1,0:T(8,128)(2,1)S(1)}, u32[]{:S(2)}, u32[]{:S(2)}) collective-permute-start(bf16[512,256]{1,0:T(8,128)(2,1)S(1)} %collective-permute-done.12), channel_id=1, source_target_pairs={{1,0},{2,1},{3,2},{4,3},{5,4},{6,5},{7,6},{8,7},{9,8},{10,9},{11,1... | collective-permute-start | bytes 786440 | tf_op jit(solution)/shard_map/ppermute | solution.py:27
  67.6 10.7 %collective-permute-start.7 = (bf16[512,256]{1,0:T(8,128)(2,1)S(1)}, bf16[512,256]{1,0:T(8,128)(2,1)}, u32[]{:S(2)}, u32[]{:S(2)}) collective-permute-start(bf16[512,256]{1,0:T(8,128)(2,1)S(1)} %collective-permute-done.6), channel_id=1, source_target_pairs={{0,1},{1,2},{2,3},{3,4},{4,5},{5,6},{6,7},{7,8},{8,9},{9,10},{10,1... | collective-permute-start | bytes 786440 | tf_op jit(solution)/shard_map/ppermute | solution.py:25
  73.3 8.5 %collective-permute-start.14 = (bf16[512,256]{1,0:T(8,128)(2,1)S(1)}, bf16[512,256]{1,0:T(8,128)(2,1)S(1)}, u32[]{:S(2)}, u32[]{:S(2)}) collective-permute-start(bf16[512,256]{1,0:T(8,128)(2,1)S(1)} %collective-permute-done.13), channel_id=1, source_target_pairs={{1,0},{2,1},{3,2},{4,3},{5,4},{6,5},{7,6},{8,7},{9,8},{10,9},{11,1... | collective-permute-start | bytes 786440 | tf_op jit(solution)/shard_map/ppermute | solution.py:27
  78.3 8.8 %collective-permute-start.8 = (bf16[512,256]{1,0:T(8,128)(2,1)}, bf16[512,256]{1,0:T(8,128)(2,1)}, u32[]{:S(2)}, u32[]{:S(2)}) collective-permute-start(bf16[512,256]{1,0:T(8,128)(2,1)} %collective-permute-done.7), channel_id=1, source_target_pairs={{0,1},{1,2},{2,3},{3,4},{4,5},{5,6},{6,7},{7,8},{8,9},{9,10},{10,1... | collective-permute-start | bytes 786440 | tf_op jit(solution)/shard_map/ppermute | solution.py:25
  81.8 18.0 %collective-permute-start.15 = (bf16[512,256]{1,0:T(8,128)(2,1)S(1)}, bf16[512,256]{1,0:T(8,128)(2,1)S(1)}, u32[]{:S(2)}, u32[]{:S(2)}) collective-permute-start(bf16[512,256]{1,0:T(8,128)(2,1)S(1)} %collective-permute-done.14), channel_id=1, source_target_pairs={{1,0},{2,1},{3,2},{4,3},{5,4},{6,5},{7,6},{8,7},{9,8},{10,9},{11,1... | collective-permute-start | bytes 786440 | tf_op jit(solution)/shard_map/ppermute | solution.py:27
  105.5 4.7 %copy-start.2 = (bf16[1,128,8192]{2,1,0:T(8,128)(2,1)S(1)}, bf16[1,128,8192]{2,1,0:T(8,128)(2,1)}, u32[]{:S(2)}) copy-start(bf16[1,128,8192]{2,1,0:T(8,128)(2,1)} %param.8) | copy-start | bytes 6291460
  105.5 4.7 %copy-start.4 = (f32[1,8192]{1,0:T(1,128)S(1)}, f32[1,8192]{1,0:T(1,128)}, u32[]{:S(2)}) copy-start(f32[1,8192]{1,0:T(1,128)} %param.11) | copy-start | bytes 98308
  105.5 4.7 %copy-start.6 = (s32[128]{0:T(128)S(1)}, s32[128]{0:T(128)}, u32[]{:S(2)}) copy-start(s32[128]{0:T(128)} %param.10) | copy-start | bytes 1540
  110.6 3.4 copy-start.1
  114.1 3.4 copy-start
  122.0 11.1 %collective-permute-start = (bf16[32,8192]{1,0:T(8,128)(2,1)S(1)}, bf16[32,8192]{1,0:T(8,128)(2,1)S(1)}, u32[]{:S(2)}, u32[]{:S(2)}) collective-permute-start(bf16[32,8192]{1,0:T(8,128)(2,1)S(1)} %get-tuple-element.590), channel_id=1, source_target_pairs={{16,0},{17,1},{18,2},{19,3},{20,4},{21,5},{22,6},{23,7},{24,8},{25... | collective-permute-start | bytes 1572872 | tf_op jit(solution)/shard_map/while/body/eval_jaxpr/ppermute | solution.py:37
  133.4 3.4 copy-start.1
  136.8 3.4 copy-start
  144.7 11.1 %collective-permute-start = (bf16[32,8192]{1,0:T(8,128)(2,1)S(1)}, bf16[32,8192]{1,0:T(8,128)(2,1)S(1)}, u32[]{:S(2)}, u32[]{:S(2)}) collective-permute-start(bf16[32,8192]{1,0:T(8,128)(2,1)S(1)} %get-tuple-element.590), channel_id=1, source_target_pairs={{16,0},{17,1},{18,2},{19,3},{20,4},{21,5},{22,6},{23,7},{24,8},{25... | collective-permute-start | bytes 1572872 | tf_op jit(solution)/shard_map/while/body/eval_jaxpr/ppermute | solution.py:37
  156.1 3.4 copy-start.1
  159.6 3.4 copy-start
  167.5 11.1 %collective-permute-start = (bf16[32,8192]{1,0:T(8,128)(2,1)S(1)}, bf16[32,8192]{1,0:T(8,128)(2,1)S(1)}, u32[]{:S(2)}, u32[]{:S(2)}) collective-permute-start(bf16[32,8192]{1,0:T(8,128)(2,1)S(1)} %get-tuple-element.590), channel_id=1, source_target_pairs={{16,0},{17,1},{18,2},{19,3},{20,4},{21,5},{22,6},{23,7},{24,8},{25... | collective-permute-start | bytes 1572872 | tf_op jit(solution)/shard_map/while/body/eval_jaxpr/ppermute | solution.py:37
  178.9 3.4 copy-start.1
  182.3 3.4 copy-start
  190.2 11.1 %collective-permute-start = (bf16[32,8192]{1,0:T(8,128)(2,1)S(1)}, bf16[32,8192]{1,0:T(8,128)(2,1)S(1)}, u32[]{:S(2)}, u32[]{:S(2)}) collective-permute-start(bf16[32,8192]{1,0:T(8,128)(2,1)S(1)} %get-tuple-element.590), channel_id=1, source_target_pairs={{16,0},{17,1},{18,2},{19,3},{20,4},{21,5},{22,6},{23,7},{24,8},{25... | collective-permute-start | bytes 1572872 | tf_op jit(solution)/shard_map/while/body/eval_jaxpr/ppermute | solution.py:37
  201.6 3.4 copy-start.1
  205.0 3.4 copy-start
  213.0 11.1 %collective-permute-start = (bf16[32,8192]{1,0:T(8,128)(2,1)S(1)}, bf16[32,8192]{1,0:T(8,128)(2,1)S(1)}, u32[]{:S(2)}, u32[]{:S(2)}) collective-permute-start(bf16[32,8192]{1,0:T(8,128)(2,1)S(1)} %get-tuple-element.590), channel_id=1, source_target_pairs={{16,0},{17,1},{18,2},{19,3},{20,4},{21,5},{22,6},{23,7},{24,8},{25... | collective-permute-start | bytes 1572872 | tf_op jit(solution)/shard_map/while/body/eval_jaxpr/ppermute | solution.py:37
  224.0 5.0 %copy-start.3 = (bf16[128,8192]{1,0:T(8,128)(2,1)S(1)}, bf16[128,8192]{1,0:T(8,128)(2,1)}, u32[]{:S(2)}) copy-start(bf16[128,8192]{1,0:T(8,128)(2,1)} %get-tuple-element.371) | copy-start | bytes 6291460
  240.0 0.7 copy-start.7
Sparse Core Ops, SparseCore 0:
  10.2 66.4 all-gather.2
  240.1 119.4 reduce-scatter.1
